TPU v7x, 256 devices: a whole 4x4x8 slice. The times are simulated.
256 devices in a mesh: dp: 16 (over z, y_lo), dep: 4 (over x), hgt: 4 (over y_hi, core).
Axes of the slice: x: 4, y: 4 (y_hi: 2, y_lo: 2; y = y_hi * 2 + y_lo), z: 8, core: 2. Of those that a mesh axis runs over, the one named last changes fastest.
Arguments:
- volume: bfloat16 [16, 32, 8, 32, 128], P('dp', None, 'dep', 'hgt'), may hold values from -6 to 6
- kernel_first: bfloat16 [27, 64, 32], replicated, may hold values from -0.21875 to 0.21875
- kernel_second: bfloat16 [27, 128, 64], replicated, may hold values from -0.15625 to 0.15625
- cotangent: bfloat16 [16, 128, 8, 32, 128], P('dp', None, 'dep', 'hgt'), may hold values from -0.01171875 to 0.01171875
Outputs:
- features: bfloat16 [16, 128, 8, 32, 128], P('dp', None, 'dep', 'hgt')
- grad_first: float32 [27, 64, 32], P(None, 'dp')
- grad_second: float32 [27, 128, 64], P(None, 'dp')
All inputs are finite; a program needn't handle non-finite values.
Results may differ from a plain program's by a relative error of at most 0.0049.
Values may be sent and summed in bfloat16 or wider, within the bound.
A program may use at most 64 MiB of HBM per device.

v0:
```python
import jax
import jax.numpy as jnp
from jax import lax
from jax.sharding import PartitionSpec as P

OFFSETS = [
    (first, second, third) for first in (-1, 0, 1) for second in (-1, 0, 1) for third in (-1, 0, 1)
]


def extended_2(x, sides, width):
    for axis, dim in sides:
        size, length = (lax.axis_size(axis), x.shape[dim])
        up = [(i, (i + 1) % size) for i in range(size - 1)]
        down = [(j, i) for i, j in up]
        last = lax.slice_in_dim(x, length - width, length, axis=dim)
        leading = lax.slice_in_dim(x, 0, width, axis=dim)
        before = lax.ppermute(last, axis, up)
        after = lax.ppermute(leading, axis, down)
        x = jnp.concatenate([before, x, after], axis=dim)
    return x


def widen(field):
    return jnp.pad(field, ((0, 0), (0, 0), (0, 0), (0, 0), (1, 1)))


def window(padded, shift_d, shift_h, shift_w, depth, height, width):
    return padded[
        :,
        :,
        1 + shift_d : 1 + shift_d + depth,
        1 + shift_h : 1 + shift_h + height,
        1 + shift_w : 1 + shift_w + width,
    ]


def convolve(extended, kernel, depth, height, width):
    padded = widen(extended)
    total = None
    for number, shift in enumerate(OFFSETS):
        piece = window(padded, shift[0], shift[1], shift[2], depth, height, width)
        term = jnp.einsum(
            "oi,bidhw->bodhw", kernel[number], piece, preferred_element_type=jnp.float32
        )
        total = term if total is None else total + term
    return total


def kernel_grad(upstream, extended, depth, height, width):
    padded = widen(extended)
    parts = []
    for shift in OFFSETS:
        piece = window(padded, shift[0], shift[1], shift[2], depth, height, width)
        parts.append(
            jnp.einsum("bodhw,bidhw->oi", upstream, piece, preferred_element_type=jnp.float32)
        )
    return jnp.stack(parts)


def per_device(volume, kernel_first, kernel_second, cotangent):
    depth, height, width = (volume.shape[2], volume.shape[3], volume.shape[4])
    vol_rim = extended_2(volume, (("dep", 2), ("hgt", 3)), 1)
    pre = convolve(vol_rim, kernel_first, depth, height, width)
    hidden = jax.nn.silu(pre).astype(jnp.bfloat16)
    hidden_rim = extended_2(hidden, (("dep", 2), ("hgt", 3)), 1)
    features = convolve(hidden_rim, kernel_second, depth, height, width).astype(jnp.bfloat16)
    cot_rim = extended_2(cotangent, (("dep", 2), ("hgt", 3)), 1)
    grad_second = kernel_grad(cotangent, hidden_rim, depth, height, width)
    padded_cot = widen(cot_rim)
    back = None
    for number, shift in enumerate(OFFSETS):
        piece = window(padded_cot, -shift[0], -shift[1], -shift[2], depth, height, width)
        term = jnp.einsum(
            "oi,bodhw->bidhw", kernel_second[number], piece, preferred_element_type=jnp.float32
        )
        back = term if back is None else back + term
    sigma = jax.nn.sigmoid(pre)
    delta = (back * (sigma * (1.0 + pre * (1.0 - sigma)))).astype(jnp.bfloat16)
    grad_first = kernel_grad(delta, vol_rim, depth, height, width)
    summed = lax.psum((grad_first, grad_second), ("dep", "hgt"))
    grad_first, grad_second = (
        lax.psum_scatter(summed[0], "dp", scatter_dimension=1, tiled=True),
        lax.psum_scatter(summed[1], "dp", scatter_dimension=1, tiled=True),
    )
    return (features, grad_first, grad_second)


def solution(mesh):
    placed = (P("dp", None, "dep", "hgt", None), P(), P(), P("dp", None, "dep", "hgt", None))
    return jax.shard_map(
        per_device,
        mesh=mesh,
        in_specs=placed,
        out_specs=(P("dp", None, "dep", "hgt", None), P(None, "dp", None), P(None, "dp", None)),
        check_vma=False,
    )
```

profile of v0, /device:TPU:8, one launch (start us, length us, event | category | flops | bytes accessed | tf_op | source)
XLA Modules:
  0.0 418.0 jit_solution(17139515704096667886)
XLA Ops:
  7.2 0.9 copy.50
  8.2 3.5 collective-permute-start
  11.7 1.4 collective-permute-start.1
  13.2 1.2 copy.56
  14.4 4.6 %collective-permute-start.8 = (bf16[1,128,1,8,128]{4,1,3,2,0:T(8,128)(2,1)S(1)}, bf16[1,128,1,8,128]{4,1,3,2,0:T(8,128)(2,1)S(1)}, u32[]{:S(2)}, u32[]{:S(2)}) collective-permute-start(bf16[1,128,1,8,128]{4,1,3,2,0:T(8,128)(2,1)S(1)} %get-tuple-element.14), channel_id=1, source_target_pairs={{0,4},{4,8},{8,12},{1,5},{5,9},{9,13},{2,6},{6,10},{10,14},{3,7},{... | collective-permute-start | bytes 786440 | tf_op jit(solution)/shard_map/ppermute | solution.py:18
  19.0 1.3 collective-permute-start.9
  20.4 1.3 collective-permute-start.2
  21.7 1.3 collective-permute-start.3
  23.3 4.0 collective-permute-done.3
  35.5 4.6 %collective-permute-start.4 = (bf16[1,64,1,8,128]{4,1,3,2,0:T(8,128)(2,1)S(1)}, bf16[1,64,1,8,128]{4,1,3,2,0:T(8,128)(2,1)S(1)}, u32[]{:S(2)}, u32[]{:S(2)}) collective-permute-start(bf16[1,64,1,8,128]{4,1,3,2,0:T(8,128)(2,1)S(1)} %get-tuple-element.19), channel_id=1, source_target_pairs={{0,4},{4,8},{8,12},{1,5},{5,9},{9,13},{2,6},{6,10},{10,14},{3,7},{... | collective-permute-start | bytes 393224 | tf_op jit(solution)/shard_map/ppermute | solution.py:18
  40.1 1.3 collective-permute-start.5
  41.6 0.9 collective-permute-done.4
  42.6 4.4 %collective-permute-done.5 = bf16[1,64,1,8,128]{4,1,3,2,0:T(8,128)(2,1)S(1)} collective-permute-done((bf16[1,64,1,8,128]{4,1,3,2,0:T(8,128)(2,1)S(1)}, bf16[1,64,1,8,128]{4,1,3,2,0:T(8,128)(2,1)S(1)}, u32[]{:S(2)}, u32[]{:S(2)}) %collective-permute-start.5) | collective-permute-done | bytes 131104 | tf_op jit(solution)/shard_map/ppermute | solution.py:19
  47.0 4.6 %collective-permute-start.6 = (bf16[1,64,4,1,128]{4,1,3,2,0:T(8,128)(2,1)S(1)}, bf16[1,64,4,1,128]{4,1,3,2,0:T(8,128)(2,1)S(1)}, u32[]{:S(2)}, u32[]{:S(2)}) collective-permute-start(bf16[1,64,4,1,128]{4,1,3,2,0:T(8,128)(2,1)S(1)} %get-tuple-element.17), channel_id=1, source_target_pairs={{0,1},{1,2},{2,3},{4,5},{5,6},{6,7},{8,9},{9,10},{10,11},{12,13},{... | collective-permute-start | bytes 196616 | tf_op jit(solution)/shard_map/ppermute | solution.py:18
  51.6 1.3 collective-permute-start.7
  53.5 4.0 collective-permute-start.10
  57.5 1.5 collective-permute-start.11
  60.0 0.9 fusion.85
  61.7 1.5 convolution_bitcast_fusion
  63.3 1.3 convolution_bitcast_fusion.7
  64.7 0.9 fusion.84
  65.6 1.0 fusion.83
  68.4 0.9 fusion.80
  69.3 0.9 fusion.79
  70.3 1.3 convolution_bitcast_fusion.1
  72.5 1.0 fusion.77
  74.4 0.9 fusion.75
  75.3 0.9 fusion.74
  76.2 0.9 fusion.73
  77.2 0.9 fusion.72
  78.1 0.9 fusion.71
  79.0 0.9 fusion.70
  80.8 0.9 fusion.68
  81.8 0.9 fusion.67
  83.6 0.9 fusion.65
  85.5 0.9 fusion.63
  86.4 1.0 fusion.62
  87.3 0.9 fusion.61
  88.3 0.9 fusion.60
  89.2 0.9 fusion.59
  92.3 1.5 convolution_add_fusion.7
  93.8 1.3 convolution_bitcast_fusion.2
  95.1 1.4 convolution_bitcast_fusion.3
  96.6 1.7 fusion.5
  111.9 1.8 copy.63
  113.8 2.1 convolution_bitcast_fusion.5
  115.9 4.0 copy.91
  120.0 2.3 convolution_bitcast_fusion.6
  122.3 2.1 convolution_add_fusion.6
  124.7 2.1 convolution_bitcast_fusion.8
  126.8 2.2 convolution_bitcast_fusion.9
  129.0 1.3 convolution_add_fusion.5
  130.3 1.2 convolution_add_fusion.4
  131.5 1.1 convolution_add_fusion.3
  132.6 1.1 convolution_add_fusion.2
  133.7 1.2 convolution_add_fusion.1
  134.9 1.1 fusion.7
  135.9 53.8 %reduce-scatter.3.cloned.1.call-done = f32[27,4,32]{2,0,1:T(8,128)} async-done(((f32[27,64,32]{2,0,1:T(8,128)}), f32[27,4,32]{2,0,1:T(8,128)}) %reduce-scatter.3.cloned.1.call-update) | async-done | bytes 13840 | tf_op jit(solution)/shard_map/reduce_scatter | solution.py:83
  189.8 76.9 %reduce-scatter.5.cloned.1.call-done = f32[27,8,64]{2,0,1:T(8,128)} async-done(((f32[27,128,64]{2,0,1:T(8,128)}), f32[27,8,64]{2,0,1:T(8,128)}) %reduce-scatter.5.cloned.1.call-update) | async-done | bytes 55312 | tf_op jit(solution)/shard_map/reduce_scatter | solution.py:84
  266.7 4.5 %fusion.27 = bf16[1,128,2,8,128]{1,4,3,2,0:T(8,128)(2,1)S(1)} fusion(f32[1,128,2,8,128]{1,4,3,2,0:T(8,128)} %convolution_bitcast_fusion, f32[1,128,2,8,128]{1,4,3,2,0:T(8,128)} %convolution_bitcast_fusion.1, f32[1,128,2,8,128]{1,4,3,2,0:T(8,128)} %convolution_bitcast_fusion.2, f32[1,128,2,8,128]{1,4,3,2,0:T(8,128)} %convolution_bitcast_fusion.3, ...), kind=kOutput, calls=%fused_computation.64 | convolution fusion | flops 36700160 | bytes 12337152 | tf_op jit(solution)/shard_map/oi,bidhw->bodhw/dot_general | solution.py:43
  271.2 1.2 copy.92
  272.4 136.0 %all-reduce.6.cloned.1.call-done = (f32[27,4,32]{2,0,1:T(8,128)}, f32[27,8,64]{2,0,1:T(8,128)}) async-done(((f32[27,4,32]{2,0,1:T(8,128)}, f32[27,8,64]{2,0,1:T(8,128)}), (f32[27,4,32]{2,0,1:T(8,128)}, f32[27,8,64]{2,0,1:T(8,128)})) %all-reduce.6.cloned.1.call-update) | async-done | bytes 69136 | tf_op jit(solution)/shard_map/psum | solution.py:81
  408.4 1.6 copy.94
  410.0 1.5 copy.93
  (143 shorter events, 33.7 us)
Async XLA Ops:
  7.2 182.6 %reduce-scatter.3.cloned.1.call-start = ((), (), s32[]{:S(2)}) async-start(), calls=%async_computation.2 | async-start | bytes 1114112 | tf_op jit(solution)/shard_map/reduce_scatter | solution.py:83
  8.2 12.1 %copy-start.5 = (bf16[1,32,2,8,128]{4,3,2,1,0:T(8,128)(2,1)S(1)}, bf16[1,32,2,8,128]{4,3,2,1,0:T(8,128)(2,1)}, u32[]{:S(2)}) copy-start(bf16[1,32,2,8,128]{4,3,2,1,0:T(8,128)(2,1)} %param.4) | copy-start | bytes 393220
  8.2 12.1 %collective-permute-start = (bf16[1,32,1,8,128]{4,1,3,2,0:T(8,128)(2,1)S(1)}, bf16[1,32,1,8,128]{4,1,3,2,0:T(8,128)(2,1)S(1)}, u32[]{:S(2)}, u32[]{:S(2)}) collective-permute-start(bf16[1,32,1,8,128]{4,1,3,2,0:T(8,128)(2,1)S(1)} %get-tuple-element.24), channel_id=1, source_target_pairs={{0,4},{4,8},{8,12},{1,5},{5,9},{9,13},{2,6},{6,10},{10,14},{3,7},{... | collective-permute-start | bytes 196616 | tf_op jit(solution)/shard_map/ppermute | solution.py:18
  11.7 11.3 %copy-start.7 = (bf16[27,64,32]{1,2,0:T(8,128)(2,1)S(1)}, bf16[27,64,32]{1,2,0:T(8,128)(2,1)}, u32[]{:S(2)}) copy-start(bf16[27,64,32]{1,2,0:T(8,128)(2,1)} %param.5) | copy-start | bytes 331780
  11.7 8.6 %collective-permute-start.1 = (bf16[1,32,1,8,128]{4,1,3,2,0:T(8,128)(2,1)S(1)}, bf16[1,32,1,8,128]{4,1,3,2,0:T(8,128)(2,1)S(1)}, u32[]{:S(2)}, u32[]{:S(2)}) collective-permute-start(bf16[1,32,1,8,128]{4,1,3,2,0:T(8,128)(2,1)S(1)} %get-tuple-element.23), channel_id=1, source_target_pairs={{4,0},{8,4},{12,8},{5,1},{9,5},{13,9},{6,2},{10,6},{14,10},{7,3},{... | collective-permute-start | bytes 196616 | tf_op jit(solution)/shard_map/ppermute | solution.py:19
  14.4 38.8 %collective-permute-start.8 = (bf16[1,128,1,8,128]{4,1,3,2,0:T(8,128)(2,1)S(1)}, bf16[1,128,1,8,128]{4,1,3,2,0:T(8,128)(2,1)S(1)}, u32[]{:S(2)}, u32[]{:S(2)}) collective-permute-start(bf16[1,128,1,8,128]{4,1,3,2,0:T(8,128)(2,1)S(1)} %get-tuple-element.14), channel_id=1, source_target_pairs={{0,4},{4,8},{8,12},{1,5},{5,9},{9,13},{2,6},{6,10},{10,14},{3,7},{... | collective-permute-start | bytes 786440 | tf_op jit(solution)/shard_map/ppermute | solution.py:18
  19.0 34.5 %collective-permute-start.9 = (bf16[1,128,1,8,128]{4,1,3,2,0:T(8,128)(2,1)S(1)}, bf16[1,128,1,8,128]{4,1,3,2,0:T(8,128)(2,1)S(1)}, u32[]{:S(2)}, u32[]{:S(2)}) collective-permute-start(bf16[1,128,1,8,128]{4,1,3,2,0:T(8,128)(2,1)S(1)} %get-tuple-element.13), channel_id=1, source_target_pairs={{4,0},{8,4},{12,8},{5,1},{9,5},{13,9},{6,2},{10,6},{14,10},{7,3},{... | collective-permute-start | bytes 786440 | tf_op jit(solution)/shard_map/ppermute | solution.py:19
  20.4 2.9 collective-permute-start.2
  21.7 5.6 %collective-permute-start.3 = (bf16[1,32,4,1,128]{4,1,3,2,0:T(8,128)(2,1)S(1)}, bf16[1,32,4,1,128]{4,1,3,2,0:T(8,128)(2,1)S(1)}, u32[]{:S(2)}, u32[]{:S(2)}) collective-permute-start(bf16[1,32,4,1,128]{4,1,3,2,0:T(8,128)(2,1)S(1)} %get-tuple-element.22), channel_id=1, source_target_pairs={{1,0},{2,1},{3,2},{5,4},{6,5},{7,6},{9,8},{10,9},{11,10},{13,12},{... | collective-permute-start | bytes 98312 | tf_op jit(solution)/shard_map/ppermute | solution.py:19
  34.9 6.5 %copy-start = (bf16[1,128,2,8,128]{4,3,2,1,0:T(8,128)(2,1)S(1)}, bf16[1,128,2,8,128]{4,3,2,1,0:T(8,128)(2,1)}, u32[]{:S(2)}) copy-start(bf16[1,128,2,8,128]{4,3,2,1,0:T(8,128)(2,1)} %param.7) | copy-start | bytes 1572868
  34.9 6.5 %copy-start.6 = (bf16[27,128,64]{1,2,0:T(8,128)(2,1)S(1)}, bf16[27,128,64]{1,2,0:T(8,128)(2,1)}, u32[]{:S(2)}) copy-start(bf16[27,128,64]{1,2,0:T(8,128)(2,1)} %param.6) | copy-start | bytes 1327108
  35.5 7.1 %collective-permute-start.4 = (bf16[1,64,1,8,128]{4,1,3,2,0:T(8,128)(2,1)S(1)}, bf16[1,64,1,8,128]{4,1,3,2,0:T(8,128)(2,1)S(1)}, u32[]{:S(2)}, u32[]{:S(2)}) collective-permute-start(bf16[1,64,1,8,128]{4,1,3,2,0:T(8,128)(2,1)S(1)} %get-tuple-element.19), channel_id=1, source_target_pairs={{0,4},{4,8},{8,12},{1,5},{5,9},{9,13},{2,6},{6,10},{10,14},{3,7},{... | collective-permute-start | bytes 393224 | tf_op jit(solution)/shard_map/ppermute | solution.py:18
  40.1 6.9 %collective-permute-start.5 = (bf16[1,64,1,8,128]{4,1,3,2,0:T(8,128)(2,1)S(1)}, bf16[1,64,1,8,128]{4,1,3,2,0:T(8,128)(2,1)S(1)}, u32[]{:S(2)}, u32[]{:S(2)}) collective-permute-start(bf16[1,64,1,8,128]{4,1,3,2,0:T(8,128)(2,1)S(1)} %get-tuple-element.20), channel_id=1, source_target_pairs={{4,0},{8,4},{12,8},{5,1},{9,5},{13,9},{6,2},{10,6},{14,10},{7,3},{... | collective-permute-start | bytes 393224 | tf_op jit(solution)/shard_map/ppermute | solution.py:19
  47.0 12.2 %collective-permute-start.6 = (bf16[1,64,4,1,128]{4,1,3,2,0:T(8,128)(2,1)S(1)}, bf16[1,64,4,1,128]{4,1,3,2,0:T(8,128)(2,1)S(1)}, u32[]{:S(2)}, u32[]{:S(2)}) collective-permute-start(bf16[1,64,4,1,128]{4,1,3,2,0:T(8,128)(2,1)S(1)} %get-tuple-element.17), channel_id=1, source_target_pairs={{0,1},{1,2},{2,3},{4,5},{5,6},{6,7},{8,9},{9,10},{10,11},{12,13},{... | collective-permute-start | bytes 196616 | tf_op jit(solution)/shard_map/ppermute | solution.py:18
  51.6 7.6 %collective-permute-start.7 = (bf16[1,64,4,1,128]{4,1,3,2,0:T(8,128)(2,1)S(1)}, bf16[1,64,4,1,128]{4,1,3,2,0:T(8,128)(2,1)S(1)}, u32[]{:S(2)}, u32[]{:S(2)}) collective-permute-start(bf16[1,64,4,1,128]{4,1,3,2,0:T(8,128)(2,1)S(1)} %get-tuple-element.18), channel_id=1, source_target_pairs={{1,0},{2,1},{3,2},{5,4},{6,5},{7,6},{9,8},{10,9},{11,10},{13,12},{... | collective-permute-start | bytes 196616 | tf_op jit(solution)/shard_map/ppermute | solution.py:19
  53.5 43.1 %collective-permute-start.10 = (bf16[1,128,4,1,128]{4,1,3,2,0:T(8,128)(2,1)S(1)}, bf16[1,128,4,1,128]{4,1,3,2,0:T(8,128)(2,1)S(1)}, u32[]{:S(2)}, u32[]{:S(2)}) collective-permute-start(bf16[1,128,4,1,128]{4,1,3,2,0:T(8,128)(2,1)S(1)} %get-tuple-element.11), channel_id=1, source_target_pairs={{0,1},{1,2},{2,3},{4,5},{5,6},{6,7},{8,9},{9,10},{10,11},{12,13},{... | collective-permute-start | bytes 393224 | tf_op jit(solution)/shard_map/ppermute | solution.py:18
  57.5 39.1 %collective-permute-start.11 = (bf16[1,128,4,1,128]{4,1,3,2,0:T(8,128)(2,1)S(1)}, bf16[1,128,4,1,128]{4,1,3,2,0:T(8,128)(2,1)S(1)}, u32[]{:S(2)}, u32[]{:S(2)}) collective-permute-start(bf16[1,128,4,1,128]{4,1,3,2,0:T(8,128)(2,1)S(1)} %get-tuple-element.12), channel_id=1, source_target_pairs={{1,0},{2,1},{3,2},{5,4},{6,5},{7,6},{9,8},{10,9},{11,10},{13,12},{... | collective-permute-start | bytes 393224 | tf_op jit(solution)/shard_map/ppermute | solution.py:19
  63.3 26.8 %copy-start.4 = (bf16[1,64,4,9,128]{4,1,3,2,0:T(8,128)(2,1)}, bf16[1,64,4,9,128]{4,1,3,2,0:T(8,128)(2,1)S(1)}, u32[]{:S(2)}) copy-start(bf16[1,64,4,9,128]{4,1,3,2,0:T(8,128)(2,1)S(1)} %get-tuple-element.15) | copy-start | bytes 1769476
  63.3 28.7 %copy-start.3 = (bf16[1,64,4,9,128]{4,1,3,2,0:T(8,128)(2,1)}, bf16[1,64,4,9,128]{4,1,3,2,0:T(8,128)(2,1)S(1)}, u32[]{:S(2)}) copy-start(bf16[1,64,4,9,128]{4,1,3,2,0:T(8,128)(2,1)S(1)} %get-tuple-element.16) | copy-start | bytes 1769476
  113.8 152.9 %reduce-scatter.5.cloned.1.call-start = ((), (), s32[]{:S(2)}) async-start(), calls=%async_computation.3 | async-start | bytes 2228224 | tf_op jit(solution)/shard_map/reduce_scatter | solution.py:84
  120.0 2.3 copy-start.1
  124.4 284.0 %all-reduce.6.cloned.1.call-start = ((), (), s32[]{:S(2)}) async-start(), calls=%async_computation.4 | async-start | bytes 393216 | tf_op jit(solution)/shard_map/psum | solution.py:81
  124.7 4.3 %copy-start.2 = (f32[2,8,128,128]{3,2,1,0:T(8,128)S(1)}, f32[2,8,128,128]{3,2,1,0:T(8,128)}, u32[]{:S(2)}) copy-start(f32[2,8,128,128]{3,2,1,0:T(8,128)} %convolution_add_fusion.6) | copy-start | bytes 3145732
Sparse Core Ops, SparseCore 0:
  113.9 75.8 reduce-scatter.2
  192.5 74.1 reduce-scatter.4
  269.6 138.7 all-reduce.5
where the time goes:
time: 419 us; the launch traced here: 418 us
  waiting for transfers between devices  276 us (66%)
  matrix products  80.8 us (19%)
  starting transfers between devices  31 us (7%)
  between operations  14.5 us (3%)
  local copies, waits for them, and re-layouts  12.7 us (3%)
    psum x1, waiting for transfers between devices, per_device(): summed = lax.psum((grad_first, grad_second), ('dep', 'hgt'))  136 us
    reduce_scatter x1, waiting for transfers between devices, per_device(): lax.psum_scatter(summed[1], 'dp', scatter_dimension=1, tiled=True)  76.9 us
    reduce_scatter x1, waiting for transfers between devices, per_device(): lax.psum_scatter(summed[0], 'dp', scatter_dimension=1, tiled=True)  53.8 us
    dot_general x54, matrix products, convolve(): jnp.einsum('oi,bidhw->bodhw', kernel[number], piece, preferred_element_ty...  41.9 us
    dot_general x54, matrix products, kernel_grad(): jnp.einsum('bodhw,bidhw->oi', upstream, piece, preferred_element_type=jnp...  31.1 us
    ppermute x6, starting transfers between devices, extended_2(): before = lax.ppermute(last, axis, up)  22.5 us
    ppermute x6, waiting for transfers between devices, extended_2(): after = lax.ppermute(leading, axis, down)  8.42 us
  transfers between devices with their start and end apart: 15, of which 6 were waited for; matrix products, arithmetic and copies ran while one was open for 18% of the time, Pallas kernels for 0%

commit v1 on v0

--- a/solution.py
+++ b/solution.py
@@ -78,7 +78,7 @@
     sigma = jax.nn.sigmoid(pre)
     delta = (back * (sigma * (1.0 + pre * (1.0 - sigma)))).astype(jnp.bfloat16)
     grad_first = kernel_grad(delta, vol_rim, depth, height, width)
-    summed = lax.psum((grad_first, grad_second), ("dep", "hgt"))
+    summed = jax.lax.psum(jax.lax.psum((grad_first, grad_second), "dep"), "hgt")
     grad_first, grad_second = (
         lax.psum_scatter(summed[0], "dp", scatter_dimension=1, tiled=True),
         lax.psum_scatter(summed[1], "dp", scatter_dimension=1, tiled=True),

time: 419 us -> 377 us (0.90)
  waiting for transfers between devices: 276 us -> 230 us
    psum x1 -> x2, waiting for transfers between devices: 136 us -> 90.2 us  [per_device(): summed = jax.lax.psum(jax.lax.psum((grad_first, grad_second), 'dep'), 'hgt')]
  transfers between devices with their start and end apart: 15 -> 16, of which waited for: 6 -> 7; matrix products, arithmetic and copies ran while one was open for 18% -> 20% of each run, Pallas kernels for 0% -> 0%
where the time goes in v1:
time: 377 us; the launch traced here: 373 us
  waiting for transfers between devices  230 us (61%)
  matrix products  81.6 us (22%)
  starting transfers between devices  31 us (8%)
  between operations  14.5 us (4%)
  local copies, waits for them, and re-layouts  12.7 us (3%)
    psum x2, waiting for transfers between devices, per_device(): summed = jax.lax.psum(jax.lax.psum((grad_first, grad_second), 'dep'), 'hgt')  90.2 us
    reduce_scatter x1, waiting for transfers between devices, per_device(): lax.psum_scatter(summed[1], 'dp', scatter_dimension=1, tiled=True)  76.8 us
    reduce_scatter x1, waiting for transfers between devices, per_device(): lax.psum_scatter(summed[0], 'dp', scatter_dimension=1, tiled=True)  53.9 us
    dot_general x54, matrix products, convolve(): jnp.einsum('oi,bidhw->bodhw', kernel[number], piece, preferred_element_ty...  42.6 us
    dot_general x54, matrix products, kernel_grad(): jnp.einsum('bodhw,bidhw->oi', upstream, piece, preferred_element_type=jnp...  31.1 us
    ppermute x6, starting transfers between devices, extended_2(): before = lax.ppermute(last, axis, up)  22.5 us
    ppermute x6, waiting for transfers between devices, extended_2(): after = lax.ppermute(leading, axis, down)  8.42 us
    ppermute x6, starting transfers between devices, extended_2(): after = lax.ppermute(leading, axis, down)  8.06 us
  transfers between devices with their start and end apart: 16, of which 7 were waited for; matrix products, arithmetic and copies ran while one was open for 20% of the time, Pallas kernels for 0%

profile of v1, /device:TPU:8, one launch (start us, length us, event | category | flops | bytes accessed | tf_op | source)
XLA Modules:
  0.0 373.1 jit_solution(13437642956782821404)
XLA Ops:
  7.2 0.9 copy.50
  8.2 3.5 collective-permute-start
  11.7 1.4 collective-permute-start.1
  13.2 1.2 copy.56
  14.4 4.6 %collective-permute-start.8 = (bf16[1,128,1,8,128]{4,1,3,2,0:T(8,128)(2,1)S(1)}, bf16[1,128,1,8,128]{4,1,3,2,0:T(8,128)(2,1)S(1)}, u32[]{:S(2)}, u32[]{:S(2)}) collective-permute-start(bf16[1,128,1,8,128]{4,1,3,2,0:T(8,128)(2,1)S(1)} %get-tuple-element.16), channel_id=1, source_target_pairs={{0,4},{4,8},{8,12},{1,5},{5,9},{9,13},{2,6},{6,10},{10,14},{3,7},{... | collective-permute-start | bytes 786440 | tf_op jit(solution)/shard_map/ppermute | solution.py:18
  19.0 1.3 collective-permute-start.9
  20.4 1.3 collective-permute-start.2
  21.7 1.3 collective-permute-start.3
  23.3 4.0 %collective-permute-done.3 = bf16[1,32,4,1,128]{4,1,3,2,0:T(8,128)(2,1)S(1)} collective-permute-done((bf16[1,32,4,1,128]{4,1,3,2,0:T(8,128)(2,1)S(1)}, bf16[1,32,4,1,128]{4,1,3,2,0:T(8,128)(2,1)S(1)}, u32[]{:S(2)}, u32[]{:S(2)}) %collective-permute-start.3) | collective-permute-done | bytes 32800 | tf_op jit(solution)/shard_map/ppermute | solution.py:19
  35.5 4.6 %collective-permute-start.4 = (bf16[1,64,1,8,128]{4,1,3,2,0:T(8,128)(2,1)S(1)}, bf16[1,64,1,8,128]{4,1,3,2,0:T(8,128)(2,1)S(1)}, u32[]{:S(2)}, u32[]{:S(2)}) collective-permute-start(bf16[1,64,1,8,128]{4,1,3,2,0:T(8,128)(2,1)S(1)} %get-tuple-element.21), channel_id=1, source_target_pairs={{0,4},{4,8},{8,12},{1,5},{5,9},{9,13},{2,6},{6,10},{10,14},{3,7},{... | collective-permute-start | bytes 393224 | tf_op jit(solution)/shard_map/ppermute | solution.py:18
  40.1 1.3 collective-permute-start.5
  41.6 0.9 collective-permute-done.4
  42.6 4.4 %collective-permute-done.5 = bf16[1,64,1,8,128]{4,1,3,2,0:T(8,128)(2,1)S(1)} collective-permute-done((bf16[1,64,1,8,128]{4,1,3,2,0:T(8,128)(2,1)S(1)}, bf16[1,64,1,8,128]{4,1,3,2,0:T(8,128)(2,1)S(1)}, u32[]{:S(2)}, u32[]{:S(2)}) %collective-permute-start.5) | collective-permute-done | bytes 131104 | tf_op jit(solution)/shard_map/ppermute | solution.py:19
  47.0 4.6 %collective-permute-start.6 = (bf16[1,64,4,1,128]{4,1,3,2,0:T(8,128)(2,1)S(1)}, bf16[1,64,4,1,128]{4,1,3,2,0:T(8,128)(2,1)S(1)}, u32[]{:S(2)}, u32[]{:S(2)}) collective-permute-start(bf16[1,64,4,1,128]{4,1,3,2,0:T(8,128)(2,1)S(1)} %get-tuple-element.19), channel_id=1, source_target_pairs={{0,1},{1,2},{2,3},{4,5},{5,6},{6,7},{8,9},{9,10},{10,11},{12,13},{... | collective-permute-start | bytes 196616 | tf_op jit(solution)/shard_map/ppermute | solution.py:18
  51.6 1.3 collective-permute-start.7
  53.5 4.0 %collective-permute-start.10 = (bf16[1,128,4,1,128]{4,1,3,2,0:T(8,128)(2,1)S(1)}, bf16[1,128,4,1,128]{4,1,3,2,0:T(8,128)(2,1)S(1)}, u32[]{:S(2)}, u32[]{:S(2)}) collective-permute-start(bf16[1,128,4,1,128]{4,1,3,2,0:T(8,128)(2,1)S(1)} %get-tuple-element.13), channel_id=1, source_target_pairs={{0,1},{1,2},{2,3},{4,5},{5,6},{6,7},{8,9},{9,10},{10,11},{12,13},{... | collective-permute-start | bytes 393224 | tf_op jit(solution)/shard_map/ppermute | solution.py:18
  57.5 1.5 collective-permute-start.11
  60.0 0.9 fusion.85
  61.9 1.3 convolution_bitcast_fusion.7
  64.1 0.9 fusion.83
  66.0 0.9 fusion.81
  66.9 1.0 fusion.80
  68.8 1.3 convolution_bitcast_fusion.1
  70.1 0.9 fusion.78
  71.0 1.0 fusion.77
  73.8 1.0 fusion.74
  74.7 0.9 fusion.73
  75.7 0.9 fusion.72
  76.6 1.0 fusion.71
  77.5 0.9 fusion.70
  78.5 0.9 fusion.69
  79.4 1.0 fusion.68
  81.2 0.9 fusion.66
  82.2 0.9 fusion.65
  83.1 0.9 fusion.64
  84.9 1.0 fusion.62
  85.9 0.9 fusion.61
  87.7 0.9 fusion.59
  90.9 1.5 convolution_add_fusion.7
  92.4 1.5 convolution_bitcast_fusion
  93.9 1.3 convolution_bitcast_fusion.2
  95.2 1.7 fusion.5
  110.6 1.8 copy.63
  112.5 2.2 convolution_bitcast_fusion.3
  114.6 4.0 %copy.91 = f32[27,128,64]{2,0,1:T(8,128)} copy(f32[27,128,64]{1,2,0:T(8,128)} %fusion.59) | data formatting | bytes 1769472 | tf_op jit(solution)/shard_map/stack | solution.py:58
  118.6 2.2 convolution_bitcast_fusion.5
  120.8 2.1 convolution_add_fusion.6
  123.3 2.3 convolution_bitcast_fusion.6
  125.6 2.0 convolution_bitcast_fusion.8
  127.6 1.3 convolution_add_fusion.5
  128.9 1.2 convolution_add_fusion.4
  130.1 1.1 convolution_add_fusion.3
  131.2 1.1 convolution_add_fusion.2
  132.3 1.2 convolution_add_fusion.1
  133.5 1.1 fusion.7
  134.5 53.9 %reduce-scatter.3.cloned.1.call-done = f32[27,4,32]{2,0,1:T(8,128)} async-done(((f32[27,64,32]{2,0,1:T(8,128)}), f32[27,4,32]{2,0,1:T(8,128)}) %reduce-scatter.3.cloned.1.call-update) | async-done | bytes 13840 | tf_op jit(solution)/shard_map/reduce_scatter | solution.py:83
  188.4 76.8 %reduce-scatter.5.cloned.1.call-done = f32[27,8,64]{2,0,1:T(8,128)} async-done(((f32[27,128,64]{2,0,1:T(8,128)}), f32[27,8,64]{2,0,1:T(8,128)}) %reduce-scatter.5.cloned.1.call-update) | async-done | bytes 55312 | tf_op jit(solution)/shard_map/reduce_scatter | solution.py:84
  265.4 2.2 convolution_bitcast_fusion.9
  267.5 48.3 %all-reduce.10.cloned.1.call-done = (f32[27,4,32]{2,0,1:T(8,128)}, f32[27,8,64]{2,0,1:T(8,128)}) async-done(((f32[27,4,32]{2,0,1:T(8,128)}, f32[27,8,64]{2,0,1:T(8,128)}), (f32[27,4,32]{2,0,1:T(8,128)}, f32[27,8,64]{2,0,1:T(8,128)})) %all-reduce.10.cloned.1.call-update) | async-done | bytes 69136 | tf_op jit(solution)/shard_map/psum | solution.py:81
  315.9 4.5 %fusion.27 = bf16[1,128,2,8,128]{1,4,3,2,0:T(8,128)(2,1)S(1)} fusion(f32[1,128,2,8,128]{1,4,3,2,0:T(8,128)} %convolution_bitcast_fusion, f32[1,128,2,8,128]{1,4,3,2,0:T(8,128)} %convolution_bitcast_fusion.1, f32[1,128,2,8,128]{1,4,3,2,0:T(8,128)} %convolution_bitcast_fusion.2, f32[1,128,2,8,128]{1,4,3,2,0:T(8,128)} %convolution_bitcast_fusion.3, ...), kind=kOutput, calls=%fused_computation.64 | convolution fusion | flops 36700160 | bytes 12337152 | tf_op jit(solution)/shard_map/oi,bidhw->bodhw/dot_general | solution.py:43
  320.4 1.2 copy.92
  321.6 41.9 %all-reduce.8.cloned.1.call-done = (f32[27,4,32]{2,0,1:T(8,128)}, f32[27,8,64]{2,0,1:T(8,128)}) async-done(((f32[27,4,32]{2,0,1:T(8,128)}, f32[27,8,64]{2,0,1:T(8,128)}), (f32[27,4,32]{2,0,1:T(8,128)}, f32[27,8,64]{2,0,1:T(8,128)})) %all-reduce.8.cloned.1.call-update) | async-done | bytes 69136 | tf_op jit(solution)/shard_map/psum | solution.py:81
  363.5 1.6 copy.94
  365.1 1.5 copy.93
  (146 shorter events, 34.7 us)
Async XLA Ops:
  7.2 181.3 %reduce-scatter.3.cloned.1.call-start = ((), (), s32[]{:S(2)}) async-start(), calls=%async_computation.2 | async-start | bytes 1114112 | tf_op jit(solution)/shard_map/reduce_scatter | solution.py:83
  8.2 12.1 %copy-start.5 = (bf16[1,32,2,8,128]{4,3,2,1,0:T(8,128)(2,1)S(1)}, bf16[1,32,2,8,128]{4,3,2,1,0:T(8,128)(2,1)}, u32[]{:S(2)}) copy-start(bf16[1,32,2,8,128]{4,3,2,1,0:T(8,128)(2,1)} %param.4) | copy-start | bytes 393220
  8.2 12.1 %collective-permute-start = (bf16[1,32,1,8,128]{4,1,3,2,0:T(8,128)(2,1)S(1)}, bf16[1,32,1,8,128]{4,1,3,2,0:T(8,128)(2,1)S(1)}, u32[]{:S(2)}, u32[]{:S(2)}) collective-permute-start(bf16[1,32,1,8,128]{4,1,3,2,0:T(8,128)(2,1)S(1)} %get-tuple-element.26), channel_id=1, source_target_pairs={{0,4},{4,8},{8,12},{1,5},{5,9},{9,13},{2,6},{6,10},{10,14},{3,7},{... | collective-permute-start | bytes 196616 | tf_op jit(solution)/shard_map/ppermute | solution.py:18
  11.7 11.3 %copy-start.7 = (bf16[27,64,32]{1,2,0:T(8,128)(2,1)S(1)}, bf16[27,64,32]{1,2,0:T(8,128)(2,1)}, u32[]{:S(2)}) copy-start(bf16[27,64,32]{1,2,0:T(8,128)(2,1)} %param.5) | copy-start | bytes 331780
  11.7 8.6 %collective-permute-start.1 = (bf16[1,32,1,8,128]{4,1,3,2,0:T(8,128)(2,1)S(1)}, bf16[1,32,1,8,128]{4,1,3,2,0:T(8,128)(2,1)S(1)}, u32[]{:S(2)}, u32[]{:S(2)}) collective-permute-start(bf16[1,32,1,8,128]{4,1,3,2,0:T(8,128)(2,1)S(1)} %get-tuple-element.25), channel_id=1, source_target_pairs={{4,0},{8,4},{12,8},{5,1},{9,5},{13,9},{6,2},{10,6},{14,10},{7,3},{... | collective-permute-start | bytes 196616 | tf_op jit(solution)/shard_map/ppermute | solution.py:19
  14.4 38.8 %collective-permute-start.8 = (bf16[1,128,1,8,128]{4,1,3,2,0:T(8,128)(2,1)S(1)}, bf16[1,128,1,8,128]{4,1,3,2,0:T(8,128)(2,1)S(1)}, u32[]{:S(2)}, u32[]{:S(2)}) collective-permute-start(bf16[1,128,1,8,128]{4,1,3,2,0:T(8,128)(2,1)S(1)} %get-tuple-element.16), channel_id=1, source_target_pairs={{0,4},{4,8},{8,12},{1,5},{5,9},{9,13},{2,6},{6,10},{10,14},{3,7},{... | collective-permute-start | bytes 786440 | tf_op jit(solution)/shard_map/ppermute | solution.py:18
  19.0 34.5 %collective-permute-start.9 = (bf16[1,128,1,8,128]{4,1,3,2,0:T(8,128)(2,1)S(1)}, bf16[1,128,1,8,128]{4,1,3,2,0:T(8,128)(2,1)S(1)}, u32[]{:S(2)}, u32[]{:S(2)}) collective-permute-start(bf16[1,128,1,8,128]{4,1,3,2,0:T(8,128)(2,1)S(1)} %get-tuple-element.15), channel_id=1, source_target_pairs={{4,0},{8,4},{12,8},{5,1},{9,5},{13,9},{6,2},{10,6},{14,10},{7,3},{... | collective-permute-start | bytes 786440 | tf_op jit(solution)/shard_map/ppermute | solution.py:19
  20.4 2.9 collective-permute-start.2
  21.7 5.6 %collective-permute-start.3 = (bf16[1,32,4,1,128]{4,1,3,2,0:T(8,128)(2,1)S(1)}, bf16[1,32,4,1,128]{4,1,3,2,0:T(8,128)(2,1)S(1)}, u32[]{:S(2)}, u32[]{:S(2)}) collective-permute-start(bf16[1,32,4,1,128]{4,1,3,2,0:T(8,128)(2,1)S(1)} %get-tuple-element.24), channel_id=1, source_target_pairs={{1,0},{2,1},{3,2},{5,4},{6,5},{7,6},{9,8},{10,9},{11,10},{13,12},{... | collective-permute-start | bytes 98312 | tf_op jit(solution)/shard_map/ppermute | solution.py:19
  34.9 6.5 %copy-start = (bf16[1,128,2,8,128]{4,3,2,1,0:T(8,128)(2,1)S(1)}, bf16[1,128,2,8,128]{4,3,2,1,0:T(8,128)(2,1)}, u32[]{:S(2)}) copy-start(bf16[1,128,2,8,128]{4,3,2,1,0:T(8,128)(2,1)} %param.7) | copy-start | bytes 1572868
  34.9 6.5 %copy-start.6 = (bf16[27,128,64]{1,2,0:T(8,128)(2,1)S(1)}, bf16[27,128,64]{1,2,0:T(8,128)(2,1)}, u32[]{:S(2)}) copy-start(bf16[27,128,64]{1,2,0:T(8,128)(2,1)} %param.6) | copy-start | bytes 1327108
  35.5 7.1 %collective-permute-start.4 = (bf16[1,64,1,8,128]{4,1,3,2,0:T(8,128)(2,1)S(1)}, bf16[1,64,1,8,128]{4,1,3,2,0:T(8,128)(2,1)S(1)}, u32[]{:S(2)}, u32[]{:S(2)}) collective-permute-start(bf16[1,64,1,8,128]{4,1,3,2,0:T(8,128)(2,1)S(1)} %get-tuple-element.21), channel_id=1, source_target_pairs={{0,4},{4,8},{8,12},{1,5},{5,9},{9,13},{2,6},{6,10},{10,14},{3,7},{... | collective-permute-start | bytes 393224 | tf_op jit(solution)/shard_map/ppermute | solution.py:18
  40.1 6.9 %collective-permute-start.5 = (bf16[1,64,1,8,128]{4,1,3,2,0:T(8,128)(2,1)S(1)}, bf16[1,64,1,8,128]{4,1,3,2,0:T(8,128)(2,1)S(1)}, u32[]{:S(2)}, u32[]{:S(2)}) collective-permute-start(bf16[1,64,1,8,128]{4,1,3,2,0:T(8,128)(2,1)S(1)} %get-tuple-element.22), channel_id=1, source_target_pairs={{4,0},{8,4},{12,8},{5,1},{9,5},{13,9},{6,2},{10,6},{14,10},{7,3},{... | collective-permute-start | bytes 393224 | tf_op jit(solution)/shard_map/ppermute | solution.py:19
  47.0 12.2 %collective-permute-start.6 = (bf16[1,64,4,1,128]{4,1,3,2,0:T(8,128)(2,1)S(1)}, bf16[1,64,4,1,128]{4,1,3,2,0:T(8,128)(2,1)S(1)}, u32[]{:S(2)}, u32[]{:S(2)}) collective-permute-start(bf16[1,64,4,1,128]{4,1,3,2,0:T(8,128)(2,1)S(1)} %get-tuple-element.19), channel_id=1, source_target_pairs={{0,1},{1,2},{2,3},{4,5},{5,6},{6,7},{8,9},{9,10},{10,11},{12,13},{... | collective-permute-start | bytes 196616 | tf_op jit(solution)/shard_map/ppermute | solution.py:18
  51.6 7.6 %collective-permute-start.7 = (bf16[1,64,4,1,128]{4,1,3,2,0:T(8,128)(2,1)S(1)}, bf16[1,64,4,1,128]{4,1,3,2,0:T(8,128)(2,1)S(1)}, u32[]{:S(2)}, u32[]{:S(2)}) collective-permute-start(bf16[1,64,4,1,128]{4,1,3,2,0:T(8,128)(2,1)S(1)} %get-tuple-element.20), channel_id=1, source_target_pairs={{1,0},{2,1},{3,2},{5,4},{6,5},{7,6},{9,8},{10,9},{11,10},{13,12},{... | collective-permute-start | bytes 196616 | tf_op jit(solution)/shard_map/ppermute | solution.py:19
  53.5 41.7 %collective-permute-start.10 = (bf16[1,128,4,1,128]{4,1,3,2,0:T(8,128)(2,1)S(1)}, bf16[1,128,4,1,128]{4,1,3,2,0:T(8,128)(2,1)S(1)}, u32[]{:S(2)}, u32[]{:S(2)}) collective-permute-start(bf16[1,128,4,1,128]{4,1,3,2,0:T(8,128)(2,1)S(1)} %get-tuple-element.13), channel_id=1, source_target_pairs={{0,1},{1,2},{2,3},{4,5},{5,6},{6,7},{8,9},{9,10},{10,11},{12,13},{... | collective-permute-start | bytes 393224 | tf_op jit(solution)/shard_map/ppermute | solution.py:18
  57.5 37.7 %collective-permute-start.11 = (bf16[1,128,4,1,128]{4,1,3,2,0:T(8,128)(2,1)S(1)}, bf16[1,128,4,1,128]{4,1,3,2,0:T(8,128)(2,1)S(1)}, u32[]{:S(2)}, u32[]{:S(2)}) collective-permute-start(bf16[1,128,4,1,128]{4,1,3,2,0:T(8,128)(2,1)S(1)} %get-tuple-element.14), channel_id=1, source_target_pairs={{1,0},{2,1},{3,2},{5,4},{6,5},{7,6},{9,8},{10,9},{11,10},{13,12},{... | collective-permute-start | bytes 393224 | tf_op jit(solution)/shard_map/ppermute | solution.py:19
  61.9 26.8 %copy-start.4 = (bf16[1,64,4,9,128]{4,1,3,2,0:T(8,128)(2,1)}, bf16[1,64,4,9,128]{4,1,3,2,0:T(8,128)(2,1)S(1)}, u32[]{:S(2)}) copy-start(bf16[1,64,4,9,128]{4,1,3,2,0:T(8,128)(2,1)S(1)} %get-tuple-element.17) | copy-start | bytes 1769476
  61.9 28.7 %copy-start.3 = (bf16[1,64,4,9,128]{4,1,3,2,0:T(8,128)(2,1)}, bf16[1,64,4,9,128]{4,1,3,2,0:T(8,128)(2,1)S(1)}, u32[]{:S(2)}) copy-start(bf16[1,64,4,9,128]{4,1,3,2,0:T(8,128)(2,1)S(1)} %get-tuple-element.18) | copy-start | bytes 1769476
  112.4 152.9 %reduce-scatter.5.cloned.1.call-start = ((), (), s32[]{:S(2)}) async-start(), calls=%async_computation.3 | async-start | bytes 2228224 | tf_op jit(solution)/shard_map/reduce_scatter | solution.py:84
  118.6 2.2 copy-start.1
  122.9 192.9 %all-reduce.10.cloned.1.call-start = ((), (), s32[]{:S(2)}) async-start(), calls=%async_computation.5 | async-start | bytes 393216 | tf_op jit(solution)/shard_map/psum | solution.py:81
  123.2 4.4 %copy-start.2 = (f32[2,8,128,128]{3,2,1,0:T(8,128)S(1)}, f32[2,8,128,128]{3,2,1,0:T(8,128)}, u32[]{:S(2)}) copy-start(f32[2,8,128,128]{3,2,1,0:T(8,128)} %convolution_add_fusion.6) | copy-start | bytes 3145732
  265.3 98.2 %all-reduce.8.cloned.1.call-start = ((), (), s32[]{:S(2)}) async-start(), calls=%async_computation.4 | async-start | bytes 393216 | tf_op jit(solution)/shard_map/psum | solution.py:81
Sparse Core Ops, SparseCore 0:
  112.5 75.8 reduce-scatter.2
  191.1 74.1 reduce-scatter.4
  267.8 48.0 all-reduce.9
  318.4 45.0 all-reduce.7
